TPU v7x, 32 devices: a whole 2x2x4 slice. The times are simulated.
32 devices in a mesh: seq: 8 (over z, x), head: 4 (over y, core).
Axes of the slice: x: 2, y: 2, z: 4, core: 2. Of those that a mesh axis runs over, the one named last changes fastest.
Arguments:
- queries: bfloat16 [1024, 2048], P('seq', 'head'), may hold values from -200 to 200
- keys: bfloat16 [1024, 2048], P('seq', 'head'), may hold values from -6 to 6
- values: bfloat16 [1024, 2048], P('seq', 'head'), may hold values from -6 to 6
- bucket: int32 [1024, 1], replicated, may hold values from 0 to 7; in each aligned block of 128 rows (0 to 127, 128 to 255, ...) at most 24 rows name the same one
- w_out: bfloat16 [2048, 4096], P('head'), may hold values from -0.125 to 0.125
- grad_out: bfloat16 [1024, 4096], P('seq'), may hold values from -6 to 6
Outputs:
- layer_out: bfloat16 [1024, 4096], P('seq', 'head')
- grad_queries: bfloat16 [1024, 2048], P('seq', 'head')
- grad_keys: bfloat16 [1024, 2048], P('seq', 'head')
- grad_values: bfloat16 [1024, 2048], P('seq', 'head')
- grad_weight: float32 [2048, 4096], P('head', 'seq')
Inputs may be any that keep to these rules, and one draw needn't show every extreme that they name: Bucket b belongs to the b-th index of seq; buckets b and b-1 are neighbouring tree leaves. Among the tokens of one block of 128 at most 24 share a bucket, and exactly 24 do in some block.
All inputs are finite; a program needn't handle non-finite values.
Results may differ from a plain program's by a relative error of at most 0.012.
Values may be sent and summed in bfloat16 or wider, within the bound.
A program may use at most 128 MiB of HBM per device.

v0:
```python
import math

import jax
import jax.numpy as jnp
from jax import lax
from jax.sharding import PartitionSpec as P

HSZ = 128


def passed_along(value, axis, by):
    length = lax.axis_size(axis)
    pairs = [(i, i + by) for i in range(length) if 0 <= i + by < length]
    return lax.ppermute(value, axis, pairs)


def member_table(bucket_grid, owner, slot_count):
    matches = (bucket_grid == owner).astype(jnp.int32)
    ranking = jnp.cumsum(matches, axis=1) - matches
    slot_ids = jnp.arange(slot_count, dtype=jnp.int32)
    placed = matches[:, :, None] * (ranking[:, :, None] == slot_ids[None, None, :]).astype(
        jnp.int32
    )
    sources = bucket_grid.shape[0]
    stride = bucket_grid.shape[1]
    offsets = (
        jnp.arange(sources, dtype=jnp.int32)[:, None] * stride
        + jnp.arange(stride, dtype=jnp.int32)[None, :]
    )
    where_at = jnp.sum(placed * offsets[:, :, None], axis=1).reshape(-1)
    present = jnp.sum(placed, axis=1).reshape(-1)
    return (where_at, present)


def allowed_mask(where_here, alive_here, where_before, alive_before):
    amount = where_here.shape[0]
    asking = alive_here[:, None] > 0
    inside = (where_here[None, :] <= where_here[:, None]) & (alive_here[None, :] > 0) & asking
    inside = inside | (jnp.arange(amount)[:, None] == jnp.arange(amount)[None, :])
    earlier = (where_before[None, :] <= where_here[:, None]) & (alive_before[None, :] > 0) & asking
    return jnp.concatenate([inside, earlier], axis=1)


def softmax_rows(scores, allowed):
    masked = jnp.where(allowed[None], scores, -1e30)
    largest = jnp.max(masked, axis=2, keepdims=True)
    weights = jnp.where(allowed[None], jnp.exp(masked - largest), 0.0)
    return weights / jnp.sum(weights, axis=2, keepdims=True)


def local_slots(bucket_grid, device, sources, slot_total):
    my_buckets = lax.dynamic_index_in_dim(bucket_grid, device, 0, keepdims=False)
    owners = jnp.arange(sources, dtype=jnp.int32)
    onehot = (my_buckets[:, None] == owners[None, :]).astype(jnp.int32)
    ranking = jnp.sum((jnp.cumsum(onehot, axis=0) - onehot) * onehot, axis=1)
    back_index = my_buckets * slot_total + ranking
    slot_ids = jnp.arange(slot_total, dtype=jnp.int32)
    placed = onehot[:, :, None] * (ranking[:, None, None] == slot_ids[None, None, :]).astype(
        jnp.int32
    )
    token_ids = jnp.arange(my_buckets.shape[0], dtype=jnp.int32)
    send_index = jnp.sum(placed * token_ids[:, None, None], axis=0).reshape(-1)
    send_live = jnp.sum(placed, axis=0).reshape(-1)
    return (back_index, send_index, send_live)


def owner_probs(query_rows, key_all, allowed, scaling):
    scores = (
        jnp.einsum("qgd,kgd->gqk", query_rows, key_all, preferred_element_type=jnp.float32)
        * scaling
    )
    return softmax_rows(scores, allowed)


def owner_forward(probs, value_all):
    rounded = probs.astype(jnp.bfloat16)
    attended = jnp.einsum(
        "gqk,kgd->qgd", rounded, value_all, preferred_element_type=jnp.float32
    ).astype(jnp.bfloat16)
    return (rounded, attended)


def owner_backward(probs, rounded, attended, grad_rows, query_rows, key_all, value_all, scaling):
    centre = jnp.sum(attended.astype(jnp.float32) * grad_rows.astype(jnp.float32), axis=2)
    dprobs = jnp.einsum("qgd,kgd->gqk", grad_rows, value_all, preferred_element_type=jnp.float32)
    dscores = probs * (dprobs - jnp.transpose(centre)[:, :, None])
    dround = dscores.astype(jnp.bfloat16)
    grad_query = (
        jnp.einsum("gqk,kgd->qgd", dround, key_all, preferred_element_type=jnp.float32) * scaling
    ).astype(jnp.bfloat16)
    grad_key = (
        jnp.einsum("gqk,qgd->kgd", dround, query_rows, preferred_element_type=jnp.float32) * scaling
    )
    grad_value = jnp.einsum("gqk,qgd->kgd", rounded, grad_rows, preferred_element_type=jnp.float32)
    return (grad_query, grad_key, grad_value)


def with_previous(key_rows, value_rows):
    key_before, value_before = passed_along((key_rows, value_rows), "seq", 1)
    return (
        jnp.concatenate([key_rows, key_before], axis=0),
        jnp.concatenate([value_rows, value_before], axis=0),
    )


def settle_keys(grad_key, grad_value, slot_rows):
    key_next, value_next = passed_along(
        (grad_key[slot_rows:].astype(jnp.bfloat16), grad_value[slot_rows:].astype(jnp.bfloat16)),
        "seq",
        -1,
    )
    key_total = (grad_key[:slot_rows] + key_next.astype(jnp.float32)).astype(jnp.bfloat16)
    value_total = (grad_value[:slot_rows] + value_next.astype(jnp.float32)).astype(jnp.bfloat16)
    return (key_total, value_total)


def per_device(queries, keys, values, bucket, w_out, grad_out):
    sources = lax.axis_size("seq")
    device = lax.axis_index("seq")
    token_rows = queries.shape[0]
    features = queries.shape[1]
    groups = features // HSZ
    slot_total = max(2, 3 * token_rows // (2 * sources))
    slot_rows = sources * slot_total
    scaling = 1.0 / math.sqrt(HSZ)
    bucket_grid = bucket[:, 0].reshape(sources, token_rows)
    back_index, send_index, send_live = local_slots(bucket_grid, device, sources, slot_total)
    where_here, alive_here = member_table(bucket_grid, device, slot_total)
    where_before, alive_before = member_table(bucket_grid, device - 1, slot_total)
    allowed = allowed_mask(where_here, alive_here, where_before, alive_before)
    grad_heads = lax.dot_general(
        grad_out, w_out, (((1,), (1,)), ((), ())), preferred_element_type=jnp.float32
    ).astype(jnp.bfloat16)

    def pack_rows(source):
        return jnp.take(source, send_index, axis=0) * send_live[:, None].astype(source.dtype)

    def split_heads(block):
        return block.reshape(block.shape[0], groups, HSZ)

    def flatten(block):
        return block.reshape(block.shape[0], features)

    query_rows, key_rows, value_rows = (
        lax.all_to_all(pack_rows(queries), "seq", split_axis=0, concat_axis=0, tiled=True),
        lax.all_to_all(pack_rows(keys), "seq", split_axis=0, concat_axis=0, tiled=True),
        lax.all_to_all(pack_rows(values), "seq", split_axis=0, concat_axis=0, tiled=True),
    )
    key_all, value_all = with_previous(key_rows, value_rows)
    probs = owner_probs(split_heads(query_rows), split_heads(key_all), allowed, scaling)
    rounded, attended = owner_forward(probs, split_heads(value_all))
    key_all, value_all, probs, rounded, attended = (key_all, value_all, probs, rounded, attended)
    returned = lax.all_to_all(flatten(attended), "seq", split_axis=0, concat_axis=0, tiled=True)
    grad_rows = lax.all_to_all(
        pack_rows(grad_heads), "seq", split_axis=0, concat_axis=0, tiled=True
    )
    grad_query, grad_key, grad_value = owner_backward(
        probs,
        rounded,
        attended,
        split_heads(grad_rows),
        split_heads(query_rows),
        split_heads(key_all),
        split_heads(value_all),
        scaling,
    )
    key_total, value_total = settle_keys(flatten(grad_key), flatten(grad_value), slot_rows)
    back_query, back_key, back_value = (
        lax.all_to_all(flatten(grad_query), "seq", split_axis=0, concat_axis=0, tiled=True),
        lax.all_to_all(key_total, "seq", split_axis=0, concat_axis=0, tiled=True),
        lax.all_to_all(value_total, "seq", split_axis=0, concat_axis=0, tiled=True),
    )
    attended_home = jnp.take(returned, back_index, axis=0)
    partial_value = jnp.dot(attended_home, w_out, preferred_element_type=jnp.float32)
    layer_out = lax.psum_scatter(
        partial_value.astype(jnp.bfloat16), "head", scatter_dimension=1, tiled=True
    )
    weight_terms = lax.dot_general(
        attended_home, grad_out, (((0,), (0,)), ((), ())), preferred_element_type=jnp.float32
    )
    grad_weight = lax.psum_scatter(weight_terms, "seq", scatter_dimension=1, tiled=True)
    grad_queries = jnp.take(back_query, back_index, axis=0)
    grad_keys = jnp.take(back_key, back_index, axis=0)
    grad_values = jnp.take(back_value, back_index, axis=0)
    return (layer_out, grad_queries, grad_keys, grad_values, grad_weight)


def solution(mesh):
    return jax.shard_map(
        per_device,
        mesh=mesh,
        in_specs=(
            P("seq", "head"),
            P("seq", "head"),
            P("seq", "head"),
            P(),
            P("head", None),
            P("seq", None),
        ),
        out_specs=(
            P("seq", "head"),
            P("seq", "head"),
            P("seq", "head"),
            P("seq", "head"),
            P("head", "seq"),
        ),
        check_vma=False,
    )
```

profile of v0, /device:TPU:0, one launch (start us, length us, event | category | flops | bytes accessed | tf_op | source)
XLA Modules:
  0.0 281.1 jit_solution(2058556022894525721)
XLA Ops:
  9.1 3.7 %convolution_convert_fusion.2 = bf16[128,512]{1,0:T(8,128)(2,1)S(1)} fusion(bf16[128,4096]{1,0:T(8,128)(2,1)S(1)} %copy-done, bf16[512,4096]{1,0:T(8,128)(2,1)} %param.14), kind=kOutput, calls=%fused_computation.25 | convolution fusion | flops 536936448 | bytes 5373952 | tf_op jit(solution)/shard_map/dot_general | solution.py:131
  17.9 7.3 %all-to-all-start.1 = ((bf16[8,24,512]{2,1,0:T(8,128)(2,1)}), bf16[8,24,512]{2,1,0:T(8,128)(2,1)S(1)}, u32[]{:S(2)}, u32[]{:S(2)}) async-start(bf16[8,24,512]{2,1,0:T(8,128)(2,1)} %bitcast.4), calls=%async_computation.1 | async-start | bytes 393216 | tf_op jit(solution)/shard_map/all_to_all | solution.py:145
  25.2 7.9 %all-to-all-done.1 = bf16[8,24,512]{2,1,0:T(8,128)(2,1)S(1)} async-done(((bf16[8,24,512]{2,1,0:T(8,128)(2,1)}), bf16[8,24,512]{2,1,0:T(8,128)(2,1)S(1)}, u32[]{:S(2)}, u32[]{:S(2)}) %all-to-all-start.1) | async-done | bytes 196640 | tf_op jit(solution)/shard_map/all_to_all | solution.py:145
  33.2 3.4 %all-to-all-start.2 = ((bf16[8,24,512]{2,1,0:T(8,128)(2,1)}), bf16[8,24,512]{2,1,0:T(8,128)(2,1)S(1)}, u32[]{:S(2)}, u32[]{:S(2)}) async-start(bf16[8,24,512]{2,1,0:T(8,128)(2,1)} %bitcast.5), calls=%async_computation.2 | async-start | bytes 393216 | tf_op jit(solution)/shard_map/all_to_all | solution.py:146
  37.8 6.5 %all-to-all-done.2 = bf16[8,24,512]{2,1,0:T(8,128)(2,1)S(1)} async-done(((bf16[8,24,512]{2,1,0:T(8,128)(2,1)}), bf16[8,24,512]{2,1,0:T(8,128)(2,1)S(1)}, u32[]{:S(2)}, u32[]{:S(2)}) %all-to-all-start.2) | async-done | bytes 196640 | tf_op jit(solution)/shard_map/all_to_all | solution.py:146
  44.3 3.4 %all-to-all-start = ((bf16[8,24,512]{2,1,0:T(8,128)(2,1)}), bf16[8,24,512]{2,1,0:T(8,128)(2,1)S(1)}, u32[]{:S(2)}, u32[]{:S(2)}) async-start(bf16[8,24,512]{2,1,0:T(8,128)(2,1)} %bitcast.2), calls=%async_computation | async-start | bytes 393216 | tf_op jit(solution)/shard_map/all_to_all | solution.py:147
  48.2 7.2 %all-to-all-done = bf16[8,24,512]{2,1,0:T(8,128)(2,1)S(1)} async-done(((bf16[8,24,512]{2,1,0:T(8,128)(2,1)}), bf16[8,24,512]{2,1,0:T(8,128)(2,1)S(1)}, u32[]{:S(2)}, u32[]{:S(2)}) %all-to-all-start) | async-done | bytes 196640 | tf_op jit(solution)/shard_map/all_to_all | solution.py:147
  55.4 3.4 %all-to-all-start.4 = ((bf16[8,24,512]{2,1,0:T(8,128)(2,1)}), bf16[8,24,512]{2,1,0:T(8,128)(2,1)S(1)}, u32[]{:S(2)}, u32[]{:S(2)}) async-start(bf16[8,24,512]{2,1,0:T(8,128)(2,1)} %bitcast.9), calls=%async_computation.5 | async-start | bytes 393216 | tf_op jit(solution)/shard_map/all_to_all | solution.py:154
  58.9 3.8 %collective-permute-start = (bf16[192,512]{1,0:T(8,128)(2,1)S(1)}, bf16[192,512]{1,0:T(8,128)(2,1)S(1)}, u32[]{:S(2)}, u32[]{:S(2)}) collective-permute-start(bf16[192,512]{1,0:T(8,128)(2,1)S(1)} %bitcast.59), channel_id=1, source_target_pairs={{0,4},{4,8},{8,12},{12,16},{16,20},{20,24},{24,28},{1,5},{5,9},{9,... | collective-permute-start | bytes 589832 | tf_op jit(solution)/shard_map/ppermute | solution.py:14
  62.8 3.4 %collective-permute-start.1 = (bf16[192,512]{1,0:T(8,128)(2,1)S(1)}, bf16[192,512]{1,0:T(8,128)(2,1)S(1)}, u32[]{:S(2)}, u32[]{:S(2)}) collective-permute-start(bf16[192,512]{1,0:T(8,128)(2,1)S(1)} %bitcast.58), channel_id=1, source_target_pairs={{0,4},{4,8},{8,12},{12,16},{16,20},{20,24},{24,28},{1,5},{5,9},{9,... | collective-permute-start | bytes 589832 | tf_op jit(solution)/shard_map/ppermute | solution.py:14
  67.1 2.7 collective-permute-done.1
  71.7 1.8 multiply_reduce_fusion
  74.3 6.8 %all-to-all-start.3 = ((bf16[8,24,512]{2,1,0:T(8,128)(2,1)}), bf16[8,24,512]{2,1,0:T(8,128)(2,1)S(1)}, u32[]{:S(2)}, u32[]{:S(2)}) async-start(bf16[8,24,512]{2,1,0:T(8,128)(2,1)} %all_to_all.68), calls=%async_computation.3 | async-start | bytes 393216 | tf_op jit(solution)/shard_map/all_to_all | solution.py:153
  81.2 7.7 %all-to-all-done.3 = bf16[8,24,512]{2,1,0:T(8,128)(2,1)S(1)} async-done(((bf16[8,24,512]{2,1,0:T(8,128)(2,1)}), bf16[8,24,512]{2,1,0:T(8,128)(2,1)S(1)}, u32[]{:S(2)}, u32[]{:S(2)}) %all-to-all-start.3) | async-done | bytes 196640 | tf_op jit(solution)/shard_map/all_to_all | solution.py:153
  89.7 3.9 %convolution_convert_fusion = bf16[128,4096]{1,0:T(8,128)(2,1)} fusion(bf16[512,4096]{1,0:T(8,128)(2,1)} %param.14, bf16[128,512]{1,0:T(8,128)(2,1)S(1)} %gather_fusion.3, pred[128]{0:T(512)(128)(4,1)S(1)} %get-tuple-element.13), kind=kOutput, calls=%fused_computation.9 | convolution fusion | flops 537460736 | bytes 5374080 | tf_op jit(solution)/shard_map/dot_general | solution.py:174
  93.7 4.6 %fusion.23 = f32[512,4096]{1,0:T(8,128)} fusion(bf16[128,4096]{1,0:T(8,128)(2,1)S(1)} %copy-done, bf16[128,512]{1,0:T(8,128)(2,1)S(1)} %gather_fusion.3, pred[128]{0:T(512)(128)(4,1)S(1)} %get-tuple-element.13), kind=kOutput, calls=%fused_computation.68 | convolution fusion | flops 536936448 | bytes 9568384 | tf_op jit(solution)/shard_map/dot_general | solution.py:178
  101.3 3.4 %all-to-all-start.5 = ((bf16[8,24,512]{2,1,0:T(8,128)(2,1)}), bf16[8,24,512]{2,1,0:T(8,128)(2,1)S(1)}, u32[]{:S(2)}, u32[]{:S(2)}) async-start(bf16[8,24,512]{2,1,0:T(8,128)(2,1)} %all_to_all.73), calls=%async_computation.6 | async-start | bytes 393216 | tf_op jit(solution)/shard_map/all_to_all | solution.py:169
  106.6 1.8 convolution_bitcast_fusion
  110.2 4.9 %collective-permute-done.2 = bf16[192,512]{1,0:T(8,128)(2,1)} collective-permute-done((bf16[192,512]{1,0:T(8,128)(2,1)S(1)}, bf16[192,512]{1,0:T(8,128)(2,1)}, u32[]{:S(2)}, u32[]{:S(2)}) %collective-permute-start.2) | collective-permute-done | bytes 196640 | tf_op jit(solution)/shard_map/ppermute | solution.py:14
  116.8 5.6 %all-to-all-start.6 = ((bf16[8,24,512]{2,1,0:T(8,128)(2,1)}), bf16[8,24,512]{2,1,0:T(8,128)(2,1)S(1)}, u32[]{:S(2)}, u32[]{:S(2)}) async-start(bf16[8,24,512]{2,1,0:T(8,128)(2,1)} %bitcast.16), calls=%async_computation.7 | async-start | bytes 393216 | tf_op jit(solution)/shard_map/all_to_all | solution.py:170
  123.4 6.8 %all-to-all-done.6 = bf16[8,24,512]{2,1,0:T(8,128)(2,1)S(1)} async-done(((bf16[8,24,512]{2,1,0:T(8,128)(2,1)}), bf16[8,24,512]{2,1,0:T(8,128)(2,1)S(1)}, u32[]{:S(2)}, u32[]{:S(2)}) %all-to-all-start.6) | async-done | bytes 196640 | tf_op jit(solution)/shard_map/all_to_all | solution.py:170
  130.2 3.4 %all-to-all-start.7 = ((bf16[8,24,512]{2,1,0:T(8,128)(2,1)}), bf16[8,24,512]{2,1,0:T(8,128)(2,1)S(1)}, u32[]{:S(2)}, u32[]{:S(2)}) async-start(bf16[8,24,512]{2,1,0:T(8,128)(2,1)} %bitcast.21), calls=%async_computation.8 | async-start | bytes 393216 | tf_op jit(solution)/shard_map/all_to_all | solution.py:171
  135.3 10.2 %all-to-all-done.7 = bf16[8,24,512]{2,1,0:T(8,128)(2,1)S(1)} async-done(((bf16[8,24,512]{2,1,0:T(8,128)(2,1)}), bf16[8,24,512]{2,1,0:T(8,128)(2,1)S(1)}, u32[]{:S(2)}, u32[]{:S(2)}) %all-to-all-start.7) | async-done | bytes 196640 | tf_op jit(solution)/shard_map/all_to_all | solution.py:171
  147.2 127.1 %reduce-scatter.5.cloned.1.call-done = f32[512,512]{1,0:T(8,128)} async-done(((f32[512,4096]{1,0:T(8,128)}), f32[512,512]{1,0:T(8,128)}) %reduce-scatter.5.cloned.1.call-update) | async-done | bytes 1048592 | tf_op jit(solution)/shard_map/reduce_scatter | solution.py:181
  (89 shorter events, 26.1 us)
Async XLA Ops:
  7.2 1.9 copy-start
  12.8 1.0 copy-start.1
  13.8 1.0 copy-start.2
  14.8 1.0 copy-start.3
  16.9 8.3 %copy-start.5 = (s32[1024,1]{0,1:T(1,128)S(1)}, s32[1024,1]{0,1:T(1,128)}, u32[]{:S(2)}) copy-start(s32[1024,1]{0,1:T(1,128)} %param.13) | copy-start | bytes 12292
  17.9 15.2 %all-to-all-start.1 = ((bf16[8,24,512]{2,1,0:T(8,128)(2,1)}), bf16[8,24,512]{2,1,0:T(8,128)(2,1)S(1)}, u32[]{:S(2)}, u32[]{:S(2)}) async-start(bf16[8,24,512]{2,1,0:T(8,128)(2,1)} %bitcast.4), calls=%async_computation.1 | async-start | bytes 393216 | tf_op jit(solution)/shard_map/all_to_all | solution.py:145
  33.2 11.1 %all-to-all-start.2 = ((bf16[8,24,512]{2,1,0:T(8,128)(2,1)}), bf16[8,24,512]{2,1,0:T(8,128)(2,1)S(1)}, u32[]{:S(2)}, u32[]{:S(2)}) async-start(bf16[8,24,512]{2,1,0:T(8,128)(2,1)} %bitcast.5), calls=%async_computation.2 | async-start | bytes 393216 | tf_op jit(solution)/shard_map/all_to_all | solution.py:146
  44.3 11.1 %all-to-all-start = ((bf16[8,24,512]{2,1,0:T(8,128)(2,1)}), bf16[8,24,512]{2,1,0:T(8,128)(2,1)S(1)}, u32[]{:S(2)}, u32[]{:S(2)}) async-start(bf16[8,24,512]{2,1,0:T(8,128)(2,1)} %bitcast.2), calls=%async_computation | async-start | bytes 393216 | tf_op jit(solution)/shard_map/all_to_all | solution.py:147
  55.4 11.6 %all-to-all-start.4 = ((bf16[8,24,512]{2,1,0:T(8,128)(2,1)}), bf16[8,24,512]{2,1,0:T(8,128)(2,1)S(1)}, u32[]{:S(2)}, u32[]{:S(2)}) async-start(bf16[8,24,512]{2,1,0:T(8,128)(2,1)} %bitcast.9), calls=%async_computation.5 | async-start | bytes 393216 | tf_op jit(solution)/shard_map/all_to_all | solution.py:154
  58.9 12.7 %collective-permute-start = (bf16[192,512]{1,0:T(8,128)(2,1)S(1)}, bf16[192,512]{1,0:T(8,128)(2,1)S(1)}, u32[]{:S(2)}, u32[]{:S(2)}) collective-permute-start(bf16[192,512]{1,0:T(8,128)(2,1)S(1)} %bitcast.59), channel_id=1, source_target_pairs={{0,4},{4,8},{8,12},{12,16},{16,20},{20,24},{24,28},{1,5},{5,9},{9,... | collective-permute-start | bytes 589832 | tf_op jit(solution)/shard_map/ppermute | solution.py:14
  62.8 7.0 %collective-permute-start.1 = (bf16[192,512]{1,0:T(8,128)(2,1)S(1)}, bf16[192,512]{1,0:T(8,128)(2,1)S(1)}, u32[]{:S(2)}, u32[]{:S(2)}) collective-permute-start(bf16[192,512]{1,0:T(8,128)(2,1)S(1)} %bitcast.58), channel_id=1, source_target_pairs={{0,4},{4,8},{8,12},{12,16},{16,20},{20,24},{24,28},{1,5},{5,9},{9,... | collective-permute-start | bytes 589832 | tf_op jit(solution)/shard_map/ppermute | solution.py:14
  69.9 1.7 copy-start.4
  74.3 14.5 %all-to-all-start.3 = ((bf16[8,24,512]{2,1,0:T(8,128)(2,1)}), bf16[8,24,512]{2,1,0:T(8,128)(2,1)S(1)}, u32[]{:S(2)}, u32[]{:S(2)}) async-start(bf16[8,24,512]{2,1,0:T(8,128)(2,1)} %all_to_all.68), calls=%async_computation.3 | async-start | bytes 393216 | tf_op jit(solution)/shard_map/all_to_all | solution.py:153
  81.1 66.1 %reduce-scatter.3.cloned.1.call-start = ((), (), s32[]{:S(2)}) async-start(), calls=%async_computation.10 | async-start | bytes 1310720 | tf_op jit(solution)/shard_map/reduce_scatter | solution.py:175
  93.7 180.6 %reduce-scatter.5.cloned.1.call-start = ((), (), s32[]{:S(2)}) async-start(), calls=%async_computation.11 | async-start | bytes 9437184 | tf_op jit(solution)/shard_map/reduce_scatter | solution.py:181
  101.3 15.5 %all-to-all-start.5 = ((bf16[8,24,512]{2,1,0:T(8,128)(2,1)}), bf16[8,24,512]{2,1,0:T(8,128)(2,1)S(1)}, u32[]{:S(2)}, u32[]{:S(2)}) async-start(bf16[8,24,512]{2,1,0:T(8,128)(2,1)} %all_to_all.73), calls=%async_computation.6 | async-start | bytes 393216 | tf_op jit(solution)/shard_map/all_to_all | solution.py:169
  105.3 9.8 %collective-permute-start.2 = (bf16[192,512]{1,0:T(8,128)(2,1)S(1)}, bf16[192,512]{1,0:T(8,128)(2,1)}, u32[]{:S(2)}, u32[]{:S(2)}) collective-permute-start(bf16[192,512]{1,0:T(8,128)(2,1)S(1)} %copy.39), channel_id=1, source_target_pairs={{4,0},{8,4},{12,8},{16,12},{20,16},{24,20},{28,24},{5,1},{9,5},{13... | collective-permute-start | bytes 589832 | tf_op jit(solution)/shard_map/ppermute | solution.py:14
  108.9 13.7 %collective-permute-start.3 = (bf16[192,512]{1,0:T(8,128)(2,1)S(1)}, bf16[192,512]{1,0:T(8,128)(2,1)S(1)}, u32[]{:S(2)}, u32[]{:S(2)}) collective-permute-start(bf16[192,512]{1,0:T(8,128)(2,1)S(1)} %copy.42), channel_id=1, source_target_pairs={{4,0},{8,4},{12,8},{16,12},{20,16},{24,20},{28,24},{5,1},{9,5},{13... | collective-permute-start | bytes 589832 | tf_op jit(solution)/shard_map/ppermute | solution.py:14
  116.8 13.4 %all-to-all-start.6 = ((bf16[8,24,512]{2,1,0:T(8,128)(2,1)}), bf16[8,24,512]{2,1,0:T(8,128)(2,1)S(1)}, u32[]{:S(2)}, u32[]{:S(2)}) async-start(bf16[8,24,512]{2,1,0:T(8,128)(2,1)} %bitcast.16), calls=%async_computation.7 | async-start | bytes 393216 | tf_op jit(solution)/shard_map/all_to_all | solution.py:170
  130.2 15.3 %all-to-all-start.7 = ((bf16[8,24,512]{2,1,0:T(8,128)(2,1)}), bf16[8,24,512]{2,1,0:T(8,128)(2,1)S(1)}, u32[]{:S(2)}, u32[]{:S(2)}) async-start(bf16[8,24,512]{2,1,0:T(8,128)(2,1)} %bitcast.21), calls=%async_computation.8 | async-start | bytes 393216 | tf_op jit(solution)/shard_map/all_to_all | solution.py:171
Sparse Core Ops, SparseCore 0:
  93.8 22.8 reduce-scatter.2
  120.9 153.3 reduce-scatter.4
where the time goes:
time: 282 us; the launch traced here: 281 us
  waiting for transfers between devices  181 us (64%)
  starting transfers between devices  46.5 us (16%)
  matrix products  19.8 us (7%)
  between operations  14.5 us (5%)
  local copies, waits for them, and re-layouts  12.6 us (4%)
  other arithmetic  6.68 us (2%)
    reduce_scatter x1, waiting for transfers between devices, per_device(): lax.psum_scatter(weight_terms, 'seq', scatter_dimension=1, tiled=True)  127 us
    all_to_all x1, waiting for transfers between devices, per_device(): lax.all_to_all(value_total, 'seq', split_axis=0, concat_axis=0, tiled=True)  10.2 us
    ppermute x4, starting transfers between devices, passed_along(): return lax.ppermute(value, axis, pairs)  9.8 us
    all_to_all x1, waiting for transfers between devices, per_device(): lax.all_to_all(pack_rows(queries), 'seq', split_axis=0, concat_axis=0, ti...  7.92 us
    all_to_all x1, waiting for transfers between devices, per_device(): lax.all_to_all(flatten(attended), 'seq', split_axis=0, concat_axis=0, til...  7.7 us
    ppermute x4, waiting for transfers between devices, passed_along(): return lax.ppermute(value, axis, pairs)  7.61 us
    all_to_all x1, starting transfers between devices, per_device(): lax.all_to_all(pack_rows(queries), 'seq', split_axis=0, concat_axis=0, ti...  7.28 us
    all_to_all x1, waiting for transfers between devices, per_device(): lax.all_to_all(pack_rows(values), 'seq', split_axis=0, concat_axis=0, til...  7.19 us
  transfers between devices with their start and end apart: 14, of which 9 were waited for; matrix products, arithmetic and copies ran while one was open for 7% of the time, Pallas kernels for 0%

commit v1 on v0

--- a/solution.py
+++ b/solution.py
@@ -1,8 +1,11 @@
+import functools
 import math
 
 import jax
 import jax.numpy as jnp
 from jax import lax
+from jax.experimental import pallas as pl
+from jax.experimental.pallas import tpu as pltpu
 from jax.sharding import PartitionSpec as P
 
 HSZ = 128
@@ -185,9 +188,463 @@
     return (layer_out, grad_queries, grad_keys, grad_values, grad_weight)
 
 
+MESH = pl.DeviceIdType.MESH
+NT = (((1,), (1,)), ((), ()))
+TN = (((0,), (0,)), ((), ()))
+
+
+def times(a, b, dims):
+    return lax.dot_general(a, b, dims, preferred_element_type=jnp.float32)
+
+
+def dense_kernel(
+    seqs,
+    heads,
+    q_hbm,
+    k_hbm,
+    v_hbm,
+    bcol,
+    brow,
+    w_hbm,
+    go_hbm,
+    lo_out,
+    gq_out,
+    gk_out,
+    gv_out,
+    gw_out,
+    w_buf,
+    go_buf,
+    gh_buf,
+    q_buf,
+    g_buf,
+    k_buf,
+    v_buf,
+    go_all,
+    att_all,
+    dq_send,
+    dk_acc,
+    dv_acc,
+    dk_send,
+    dv_send,
+    dq_in,
+    dk_in,
+    dv_in,
+    dk_far,
+    dv_far,
+    lo_send,
+    lo_in,
+    local_sem,
+    in_send,
+    in_recv,
+    far_send,
+    far_recv,
+    go_send,
+    go_recv,
+    gx_send,
+    gx_recv,
+    att_send,
+    att_recv,
+    attx_send,
+    attx_recv,
+    fwd_send,
+    fwd_recv,
+    dq_ssem,
+    dq_rsem,
+    dk_ssem,
+    dk_rsem,
+    dkf_ssem,
+    dkf_rsem,
+    lo_ssem,
+    lo_rsem,
+):
+    s = lax.axis_index("seq")
+    h = lax.axis_index("head")
+    rows = q_hbm.shape[0]
+    width = HSZ
+    groups = q_hbm.shape[1] // width
+    half = lax.div(s, groups)
+    mine = lax.rem(s, groups)
+    part = groups * rows
+    scaling = 1.0 / math.sqrt(HSZ)
+    gcols = w_hbm.shape[1] // seqs
+    lcols = w_hbm.shape[1] // heads
+    quarter = rows // heads
+    low = half == 0
+    high = half == 1
+
+    def near(r):
+        return lax.rem(mine + r, groups)
+
+    def rows_of(block):
+        return pl.ds(pl.multiple_of(block * rows, rows), rows)
+
+    def cols_of(block, size=width):
+        return pl.ds(pl.multiple_of(block * size, size), size)
+
+    def remote(src, dst, ssem, rsem, where):
+        return pltpu.make_async_remote_copy(
+            src_ref=src, dst_ref=dst, send_sem=ssem, recv_sem=rsem, device_id=where,
+            device_id_type=MESH,
+        )
+
+    w_copy = pltpu.make_async_copy(w_hbm, w_buf, local_sem.at[0])
+    go_copy = pltpu.make_async_copy(go_hbm, go_buf, local_sem.at[1])
+    go_copy.start()
+    w_copy.start()
+    own = [
+        pltpu.make_async_copy(k_hbm.at[:, cols_of(mine)], k_buf.at[rows_of(s), :], local_sem.at[2]),
+        pltpu.make_async_copy(v_hbm.at[:, cols_of(mine)], v_buf.at[rows_of(s), :], local_sem.at[3]),
+        pltpu.make_async_copy(q_hbm.at[:, cols_of(mine)], q_buf.at[rows_of(mine), :], local_sem.at[4]),
+    ]
+    for copy in own:
+        copy.start()
+    quarter_rows = pl.ds(pl.multiple_of(h * quarter, quarter), quarter)
+    go_own = pltpu.make_async_copy(
+        go_hbm.at[quarter_rows, cols_of(s, gcols)], go_all.at[s, quarter_rows, :], local_sem.at[5]
+    )
+    go_own.start()
+
+    barrier = pltpu.get_barrier_semaphore()
+    for r in range(1, seqs):
+        pl.semaphore_signal(
+            barrier, inc=1, device_id=(lax.rem(s + r, seqs), h), device_id_type=MESH
+        )
+    for r in range(1, heads):
+        pl.semaphore_signal(
+            barrier, inc=1, device_id=(s, lax.rem(h + r, heads)), device_id_type=MESH
+        )
+    pl.semaphore_wait(barrier, seqs + heads - 2)
+
+    far = []
+    for r in range(groups):
+        to = near(r)
+        there = ((1 - half) * groups + to, h)
+        for n, (src, dst) in enumerate(((k_hbm, k_buf), (v_hbm, v_buf))):
+            far.append(
+                remote(
+                    src.at[:, cols_of(to)], dst.at[rows_of(s), :], far_send.at[r, n],
+                    far_recv.at[r, n], there,
+                )
+            )
+
+    inside = []
+    for r in range(1, groups):
+        to = near(r)
+        there = (half * groups + to, h)
+        for n, (src, dst, at) in enumerate(
+            ((k_hbm, k_buf, s), (v_hbm, v_buf, s), (q_hbm, q_buf, mine))
+        ):
+            copy = remote(
+                src.at[:, cols_of(to)], dst.at[rows_of(at), :], in_send.at[r, n],
+                in_recv.at[r, n], there,
+            )
+            copy.start()
+            inside.append(copy)
+
+    @pl.when(low)
+    def _():
+        for copy in far:
+            copy.start()
+        k_buf[pl.ds(part, part), :] = jnp.zeros((part, width), k_buf.dtype)
+        v_buf[pl.ds(part, part), :] = jnp.zeros((part, width), v_buf.dtype)
+
+    @pl.when(high)
+    def _():
+        dk_far[...] = jnp.zeros_like(dk_far)
+        dv_far[...] = jnp.zeros_like(dv_far)
+
+    go_copy.wait()
+    w_copy.wait()
+    depth = w_buf.shape[1] // seqs
+
+    def heads_step(c, total):
+        at = pl.ds(pl.multiple_of(c * depth, depth), depth)
+        return total + times(go_buf[:, at], w_buf[:, at], NT)
+
+    gh = lax.fori_loop(
+        0, seqs, heads_step, jnp.zeros((rows, groups * width), jnp.float32)
+    )
+    gh_buf[...] = gh.astype(jnp.bfloat16)
+    for r in range(1, groups):
+        to = near(r)
+        copy = remote(
+            gh_buf.at[:, cols_of(to)], g_buf.at[rows_of(mine), :], in_send.at[r, 3],
+            in_recv.at[r, 3], (half * groups + to, h),
+        )
+        copy.start()
+        inside.append(copy)
+    g_buf[rows_of(mine), :] = gh_buf[:, cols_of(mine)]
+
+    spread = []
+    for r in range(1, seqs):
+        to = lax.rem(s + r, seqs)
+        copy = remote(
+            go_hbm.at[quarter_rows, cols_of(to, gcols)], go_all.at[s, quarter_rows, :],
+            go_send.at[r], go_recv.at[r], (to, h),
+        )
+        copy.start()
+        spread.append(copy)
+
+    for copy in own:
+        copy.wait()
+    for copy in inside:
+        copy.wait_recv()
+
+    @pl.when(high)
+    def _():
+        for copy in far:
+            copy.wait_recv()
+
+    keys_bucket = brow[...]
+    keys_at = lax.broadcasted_iota(jnp.int32, (rows, seqs * rows), 1)
+    exchange = []
+    sent = []
+    att_near = []
+    att_cross = []
+    dq_near = []
+    order = list(range(1, groups)) + [0]
+    for step, r in enumerate(order):
+        block = near(r)
+        token = half * groups + block
+        qc = q_buf[rows_of(block), :]
+        gc = g_buf[rows_of(block), :]
+        k_all = k_buf[...]
+        v_all = v_buf[...]
+        gap = bcol[rows_of(token), :] - keys_bucket
+        query_at = token * rows + lax.broadcasted_iota(jnp.int32, (rows, seqs * rows), 0)
+        allowed = ((gap == 0) | (gap == 1)) & (keys_at <= query_at)
+        scores = jnp.where(allowed, times(qc, k_all, NT) * scaling, -1e30)
+        largest = jnp.max(scores, axis=1, keepdims=True)
+        weights = jnp.where(allowed, jnp.exp(scores - largest), 0.0)
+        probs = weights * (1.0 / jnp.sum(weights, axis=1, keepdims=True))
+        rounded = probs.astype(jnp.bfloat16)
+        attended = jnp.dot(rounded, v_all, preferred_element_type=jnp.float32).astype(jnp.bfloat16)
+        att_all[rows_of(token), cols_of(mine)] = attended
+        for n in range(1, groups):
+            copy = remote(
+                att_all.at[rows_of(token), cols_of(mine)],
+                att_all.at[rows_of(token), cols_of(mine)],
+                att_send.at[step, n], att_recv.at[step, n],
+                (half * groups + near(n), h),
+            )
+            copy.start()
+            att_near.append(copy)
+        copy = remote(
+            att_all.at[rows_of(token), cols_of(mine)],
+            att_all.at[rows_of(token), cols_of(mine)],
+            attx_send.at[step], attx_recv.at[step], ((1 - half) * groups + mine, h),
+        )
+        copy.start()
+        att_cross.append(copy)
+        centre = jnp.sum(
+            attended.astype(jnp.float32) * gc.astype(jnp.float32), axis=1, keepdims=True
+        )
+        dscores = (probs * (times(gc, v_all, NT) - centre)).astype(jnp.bfloat16)
+        dq = (jnp.dot(dscores, k_all, preferred_element_type=jnp.float32) * scaling).astype(
+            jnp.bfloat16
+        )
+        if r == 0:
+            dq_in[:, cols_of(mine)] = dq
+        else:
+            dq_send[r] = dq
+            copy = remote(
+                dq_send.at[r], dq_in.at[:, cols_of(mine)], dq_ssem.at[r], dq_rsem.at[r],
+                (token, h),
+            )
+            copy.start()
+            dq_near.append(copy)
+        dk = times(dscores, qc, TN)
+        dv = times(rounded, gc, TN)
+        if step == 0:
+            dk_acc[...] = dk
+            dv_acc[...] = dv
+        else:
+            dk_acc[...] += dk
+            dv_acc[...] += dv
+        if step == 1:
+            go_own.wait()
+            for copy in spread:
+                copy.wait_recv()
+            for n in range(1, heads):
+                copy = remote(
+                    go_all.at[:, quarter_rows, :], go_all.at[:, quarter_rows, :],
+                    gx_send.at[n], gx_recv.at[n], (s, lax.rem(h + n, heads)),
+                )
+                copy.start()
+                exchange.append(copy)
+
+    dk_send[...] = (dk_acc[...] * scaling).astype(jnp.bfloat16)
+    dv_send[...] = dv_acc[...].astype(jnp.bfloat16)
+    dk_cross = []
+    for r in range(groups):
+        to = near(r)
+        for n, (src, dst) in enumerate(((dk_send, dk_far), (dv_send, dv_far))):
+            dk_cross.append(
+                remote(
+                    src.at[rows_of(to), :], dst.at[:, cols_of(mine)], dkf_ssem.at[r, n],
+                    dkf_rsem.at[r, n], ((1 - half) * groups + to, h),
+                )
+            )
+
+    @pl.when(high)
+    def _():
+        for copy in dk_cross:
+            copy.start()
+
+    dk_near = []
+    for r in range(1, groups):
+        to = near(r)
+        for n, (src, dst) in enumerate(((dk_send, dk_in), (dv_send, dv_in))):
+            copy = remote(
+                src.at[rows_of(half * groups + to), :], dst.at[:, cols_of(mine)],
+                dk_ssem.at[r, n], dk_rsem.at[r, n], (half * groups + to, h),
+            )
+            copy.start()
+            dk_near.append(copy)
+    dk_in[:, cols_of(mine)] = dk_send[rows_of(s), :]
+    dv_in[:, cols_of(mine)] = dv_send[rows_of(s), :]
+
+    for copy in att_cross:
+        copy.wait_recv()
+    forward = []
+    theirs = pl.ds(pl.multiple_of((1 - half) * part, part), part)
+    for n in range(1, groups):
+        copy = remote(
+            att_all.at[theirs, cols_of(mine)], att_all.at[theirs, cols_of(mine)],
+            fwd_send.at[n], fwd_recv.at[n], (half * groups + near(n), h),
+        )
+        copy.start()
+        forward.append(copy)
+
+    for copy in att_near:
+        copy.wait_recv()
+    home = att_all[rows_of(s), :]
+    lo_near = []
+    for n in range(1, heads):
+        to = lax.rem(h + n, heads)
+        lo_send[n] = jnp.dot(
+            home, w_buf[:, cols_of(to, lcols)], preferred_element_type=jnp.float32
+        ).astype(jnp.bfloat16)
+        copy = remote(lo_send.at[n], lo_in.at[n], lo_ssem.at[n], lo_rsem.at[n], (s, to))
+        copy.start()
+        lo_near.append(copy)
+    layer = jnp.dot(home, w_buf[:, cols_of(h, lcols)], preferred_element_type=jnp.float32)
+
+    for copy in exchange:
+        copy.wait_recv()
+    for copy in dq_near:
+        copy.wait_recv()
+    gq_out[...] = dq_in[...]
+    for n, copy in enumerate(lo_near):
+        copy.wait_recv()
+        layer = layer + lo_in[n + 1].astype(jnp.float32)
+    lo_out[...] = layer.astype(jnp.bfloat16)
+    for copy in forward:
+        copy.wait_recv()
+    gw = jnp.zeros(gw_out.shape, jnp.float32)
+    for c in range(seqs):
+        gw = gw + times(att_all[c * rows : (c + 1) * rows, :], go_all[c], TN)
+    gw_out[...] = gw
+    for copy in dk_near:
+        copy.wait_recv()
+
+    @pl.when(low)
+    def _():
+        for copy in dk_cross:
+            copy.wait_recv()
+
+    gk_out[...] = (dk_in[...].astype(jnp.float32) + dk_far[...].astype(jnp.float32)).astype(
+        jnp.bfloat16
+    )
+    gv_out[...] = (dv_in[...].astype(jnp.float32) + dv_far[...].astype(jnp.float32)).astype(
+        jnp.bfloat16
+    )
+
+    for copy in (
+        inside + spread + exchange + att_near + att_cross + dq_near + dk_near + forward + lo_near
+    ):
+        copy.wait_send()
+
+    @pl.when(low)
+    def _():
+        for copy in far:
+            copy.wait_send()
+
+    @pl.when(high)
+    def _():
+        for copy in dk_cross:
+            copy.wait_send()
+
+
+def dense_device(queries, keys, values, bucket, w_out, grad_out):
+    seqs = lax.axis_size("seq")
+    heads = lax.axis_size("head")
+    rows, features = queries.shape
+    model = w_out.shape[1]
+    groups = features // HSZ
+    part = groups * rows
+    tokens = seqs * rows
+    bf, f32 = jnp.bfloat16, jnp.float32
+    vmem = pl.BlockSpec(memory_space=pltpu.VMEM)
+    hbm = pl.BlockSpec(memory_space=pl.ANY)
+    dma = pltpu.SemaphoreType.DMA
+    wide = pltpu.VMEM((rows, features), bf)
+    sems = []
+    for shape in (
+        (groups, 4), (groups, 2), (seqs,), (heads,), (groups, groups), (groups,), (groups,),
+        (groups,), (groups, 2), (groups, 2), (heads,),
+    ):
+        sems += [dma(shape), dma(shape)]
+    return pl.pallas_call(
+        functools.partial(dense_kernel, seqs, heads),
+        out_shape=(
+            jax.ShapeDtypeStruct((rows, model // heads), bf),
+            jax.ShapeDtypeStruct((rows, features), bf),
+            jax.ShapeDtypeStruct((rows, features), bf),
+            jax.ShapeDtypeStruct((rows, features), bf),
+            jax.ShapeDtypeStruct((features, model // seqs), f32),
+        ),
+        in_specs=[hbm, hbm, hbm, vmem, vmem, hbm, hbm],
+        out_specs=(vmem,) * 5,
+        scratch_shapes=[
+            pltpu.VMEM(w_out.shape, bf),
+            pltpu.VMEM(grad_out.shape, bf),
+            wide,
+            pltpu.VMEM((part, HSZ), bf),
+            pltpu.VMEM((part, HSZ), bf),
+            pltpu.VMEM((tokens, HSZ), bf),
+            pltpu.VMEM((tokens, HSZ), bf),
+            pltpu.VMEM((seqs, rows, model // seqs), bf),
+            pltpu.VMEM((tokens, features), bf),
+            pltpu.VMEM((groups, rows, HSZ), bf),
+            pltpu.VMEM((tokens, HSZ), f32),
+            pltpu.VMEM((tokens, HSZ), f32),
+            pltpu.VMEM((tokens, HSZ), bf),
+            pltpu.VMEM((tokens, HSZ), bf),
+            wide,
+            wide,
+            wide,
+            wide,
+            wide,
+            pltpu.VMEM((heads, rows, model // heads), bf),
+            pltpu.VMEM((heads, rows, model // heads), bf),
+            dma((6,)),
+        ]
+        + sems,
+        compiler_params=pltpu.CompilerParams(collective_id=0, has_side_effects=True),
+    )(queries, keys, values, bucket, bucket.reshape(1, -1), w_out, grad_out)
+
+
+def choose(queries, keys, values, bucket, w_out, grad_out):
+    groups = queries.shape[1] // HSZ
+    dense = lax.axis_size("seq") == 2 * groups
+    plan = dense_device if dense else per_device
+    return plan(queries, keys, values, bucket, w_out, grad_out)
+
+
 def solution(mesh):
     return jax.shard_map(
-        per_device,
+        choose,
         mesh=mesh,
         in_specs=(
             P("seq", "head"),

time: 282 us -> 61.5 us (0.22)
  the two profiles are of different devices: /device:TPU:0 before, /device:TPU:1 now
where the time goes in v1:
time: 61.5 us; the launch traced here: 61.2 us
  Pallas kernels  50.2 us (82%)
  local copies, waits for them, and re-layouts  10.3 us (17%)
  between operations  0.64 us (1%)
    pallas_call x1, Pallas kernels, dense_device(): pl.pallas_call(functools.partial(dense_kernel, seqs, heads), out_shape=(j...  50.2 us
    unnamed x6, local copies, waits for them, and re-layouts  10.3 us

profile of v1, /device:TPU:1, one launch (start us, length us, event | category | flops | bytes accessed | tf_op | source)
XLA Modules:
  0.0 61.2 jit_solution(4211576042189982233)
XLA Ops:
  0.6 1.7 %copy.11.bcol = s32[1024,1]{1,0:T(8,128)} copy(s32[1024,1]{0,1:T(1,128)} %param.9) | data formatting | bytes 8192 | tf_op args[3]
  2.3 50.2 %shard_map.101 = (bf16[128,1024]{1,0:T(8,128)(2,1)}, bf16[128,512]{1,0:T(8,128)(2,1)}, bf16[128,512]{1,0:T(8,128)(2,1)}, bf16[128,512]{1,0:T(8,128)(2,1)}, f32[512,512]{1,0:T(8,128)}) custom-call(bf16[128,512]{1,0:T(8,128)(2,1)} %q_hbm.1, bf16[128,512]{1,0:T(8,128)(2,1)} %k_hbm.1, bf16[128,512]{1,0:T(8,128)(2,1)} %v_hbm.1, s32[1024,1]{1,0:T(8,128)} %copy.11.bcol, ...), custom_call_target="tpu_custom_call" | custom-call | tf_op jit(solution)/shard_map/pallas_call | solution.py:598
  52.6 1.7 %copy.17 = bf16[128,1024]{1,0:T(8,128)(2,1)} copy(bf16[128,1024]{1,0:T(8,128)(2,1)} %get-tuple-element.10) | data formatting | bytes 524288
  54.2 1.6 %copy.18 = bf16[128,512]{1,0:T(8,128)(2,1)} copy(bf16[128,512]{1,0:T(8,128)(2,1)} %get-tuple-element.11) | data formatting | bytes 262144
  55.8 1.6 %copy.19 = bf16[128,512]{1,0:T(8,128)(2,1)} copy(bf16[128,512]{1,0:T(8,128)(2,1)} %get-tuple-element.12) | data formatting | bytes 262144
  57.4 1.6 %copy.20 = bf16[128,512]{1,0:T(8,128)(2,1)} copy(bf16[128,512]{1,0:T(8,128)(2,1)} %get-tuple-element.13) | data formatting | bytes 262144
  58.9 2.3 %copy.21 = f32[512,512]{1,0:T(8,128)} copy(f32[512,512]{1,0:T(8,128)} %get-tuple-element.14) | data formatting | bytes 2097152

commit v2 on v1

--- a/solution.py
+++ b/solution.py
@@ -203,7 +203,6 @@
     q_hbm,
     k_hbm,
     v_hbm,
-    bcol,
     brow,
     w_hbm,
     go_hbm,
@@ -217,22 +216,32 @@
     gh_buf,
     q_buf,
     g_buf,
-    k_buf,
-    v_buf,
+    k_near,
+    v_near,
+    k_far,
+    v_far,
     go_all,
     att_all,
+    s_buf,
+    dp_buf,
+    p_near,
+    p_far,
+    ds_near,
+    ds_far,
     dq_send,
-    dk_acc,
-    dv_acc,
     dk_send,
     dv_send,
+    dkf_send,
+    dvf_send,
     dq_in,
     dk_in,
     dv_in,
-    dk_far,
-    dv_far,
+    dk_back,
+    dv_back,
     lo_send,
     lo_in,
+    sum_send,
+    sum_in,
     local_sem,
     in_send,
     in_recv,
@@ -242,6 +251,8 @@
     go_recv,
     gx_send,
     gx_recv,
+    gf_send,
+    gf_recv,
     att_send,
     att_recv,
     attx_send,
@@ -256,15 +267,21 @@
     dkf_rsem,
     lo_ssem,
     lo_rsem,
+    sum_ssem,
+    sum_rsem,
 ):
     s = lax.axis_index("seq")
     h = lax.axis_index("head")
+    bf, f32 = jnp.bfloat16, jnp.float32
     rows = q_hbm.shape[0]
     width = HSZ
     groups = q_hbm.shape[1] // width
     half = lax.div(s, groups)
     mine = lax.rem(s, groups)
     part = groups * rows
+    pairs = heads // 2
+    core = lax.rem(h, 2)
+    partner = h + 1 - 2 * core
     scaling = 1.0 / math.sqrt(HSZ)
     gcols = w_hbm.shape[1] // seqs
     lcols = w_hbm.shape[1] // heads
@@ -281,6 +298,9 @@
     def cols_of(block, size=width):
         return pl.ds(pl.multiple_of(block * size, size), size)
 
+    def quarter_of(head):
+        return pl.ds(pl.multiple_of(head * quarter, quarter), quarter)
+
     def remote(src, dst, ssem, rsem, where):
         return pltpu.make_async_remote_copy(
             src_ref=src, dst_ref=dst, send_sem=ssem, recv_sem=rsem, device_id=where,
@@ -292,15 +312,16 @@
     go_copy.start()
     w_copy.start()
     own = [
-        pltpu.make_async_copy(k_hbm.at[:, cols_of(mine)], k_buf.at[rows_of(s), :], local_sem.at[2]),
-        pltpu.make_async_copy(v_hbm.at[:, cols_of(mine)], v_buf.at[rows_of(s), :], local_sem.at[3]),
-        pltpu.make_async_copy(q_hbm.at[:, cols_of(mine)], q_buf.at[rows_of(mine), :], local_sem.at[4]),
+        pltpu.make_async_copy(
+            src.at[:, cols_of(mine)], dst.at[rows_of(mine), :], local_sem.at[2 + n]
+        )
+        for n, (src, dst) in enumerate(((k_hbm, k_near), (v_hbm, v_near), (q_hbm, q_buf)))
     ]
     for copy in own:
         copy.start()
-    quarter_rows = pl.ds(pl.multiple_of(h * quarter, quarter), quarter)
     go_own = pltpu.make_async_copy(
-        go_hbm.at[quarter_rows, cols_of(s, gcols)], go_all.at[s, quarter_rows, :], local_sem.at[5]
+        go_hbm.at[quarter_of(h), cols_of(s, gcols)], go_all.at[s, quarter_of(h), :],
+        local_sem.at[5],
     )
     go_own.start()
 
@@ -316,42 +337,36 @@
     pl.semaphore_wait(barrier, seqs + heads - 2)
 
     far = []
-    for r in range(groups):
-        to = near(r)
-        there = ((1 - half) * groups + to, h)
-        for n, (src, dst) in enumerate(((k_hbm, k_buf), (v_hbm, v_buf))):
+    for n, (src, dst) in enumerate(((k_hbm, k_far), (v_hbm, v_far))):
+        for r in range(groups):
+            to = near(r)
             far.append(
                 remote(
-                    src.at[:, cols_of(to)], dst.at[rows_of(s), :], far_send.at[r, n],
-                    far_recv.at[r, n], there,
+                    src.at[:, cols_of(to)], dst.at[rows_of(mine), :], far_send.at[r, n],
+                    far_recv.at[r, n], ((1 - half) * groups + to, h),
                 )
             )
-
-    inside = []
-    for r in range(1, groups):
-        to = near(r)
-        there = (half * groups + to, h)
-        for n, (src, dst, at) in enumerate(
-            ((k_hbm, k_buf, s), (v_hbm, v_buf, s), (q_hbm, q_buf, mine))
-        ):
-            copy = remote(
-                src.at[:, cols_of(to)], dst.at[rows_of(at), :], in_send.at[r, n],
-                in_recv.at[r, n], there,
-            )
-            copy.start()
-            inside.append(copy)
 
     @pl.when(low)
     def _():
         for copy in far:
             copy.start()
-        k_buf[pl.ds(part, part), :] = jnp.zeros((part, width), k_buf.dtype)
-        v_buf[pl.ds(part, part), :] = jnp.zeros((part, width), v_buf.dtype)
+
+    inside = []
+    for n, (src, dst) in enumerate(((k_hbm, k_near), (q_hbm, q_buf), (v_hbm, v_near))):
+        for r in range(1, groups):
+            to = near(r)
+            copy = remote(
+                src.at[:, cols_of(to)], dst.at[rows_of(mine), :], in_send.at[r, n],
+                in_recv.at[r, n], (half * groups + to, h),
+            )
+            copy.start()
+            inside.append(copy)
 
     @pl.when(high)
     def _():
-        dk_far[...] = jnp.zeros_like(dk_far)
-        dv_far[...] = jnp.zeros_like(dv_far)
+        dk_back[...] = jnp.zeros_like(dk_back)
+        dv_back[...] = jnp.zeros_like(dv_back)
 
     go_copy.wait()
     w_copy.wait()
@@ -361,10 +376,9 @@
         at = pl.ds(pl.multiple_of(c * depth, depth), depth)
         return total + times(go_buf[:, at], w_buf[:, at], NT)
 
-    gh = lax.fori_loop(
-        0, seqs, heads_step, jnp.zeros((rows, groups * width), jnp.float32)
-    )
-    gh_buf[...] = gh.astype(jnp.bfloat16)
+    gh = lax.fori_loop(0, seqs, heads_step, jnp.zeros((rows, groups * width), f32))
+    gh_buf[...] = gh.astype(bf)
+    inside_g = []
     for r in range(1, groups):
         to = near(r)
         copy = remote(
@@ -372,137 +386,202 @@
             in_recv.at[r, 3], (half * groups + to, h),
         )
         copy.start()
-        inside.append(copy)
+        inside_g.append(copy)
     g_buf[rows_of(mine), :] = gh_buf[:, cols_of(mine)]
 
     spread = []
     for r in range(1, seqs):
         to = lax.rem(s + r, seqs)
         copy = remote(
-            go_hbm.at[quarter_rows, cols_of(to, gcols)], go_all.at[s, quarter_rows, :],
+            go_hbm.at[quarter_of(h), cols_of(to, gcols)], go_all.at[s, quarter_of(h), :],
             go_send.at[r], go_recv.at[r], (to, h),
         )
         copy.start()
         spread.append(copy)
+
+    lanes = lax.broadcasted_iota(jnp.int32, (rows, rows), 1)
+    downs = lax.broadcasted_iota(jnp.int32, (rows, rows), 0)
+
+    def asking(token):
+        row = brow[:, cols_of(token, rows)]
+        return jnp.sum(jnp.where(lanes == downs, row, 0), axis=1, keepdims=True)
+
+    def matching(token, start):
+        gap = asking(token) - brow[:, cols_of(start, part)]
+        return (gap == 0) | (gap == 1)
 
     for copy in own:
         copy.wait()
     for copy in inside:
         copy.wait_recv()
 
+    order = list(range(1, groups)) + [0]
+    keys_at = lax.broadcasted_iota(jnp.int32, (rows, part), 1)
+    query_at = lax.broadcasted_iota(jnp.int32, (rows, part), 0)
+    for r in order:
+        block = near(r)
+        allowed = matching(half * groups + block, half) & (keys_at <= block * rows + query_at)
+        s_buf[rows_of(block), :] = jnp.where(
+            allowed, times(q_buf[rows_of(block), :], k_near[...], NT) * scaling, -1e30
+        )
+    for copy in inside_g:
+        copy.wait_recv()
+    for r in order:
+        at = rows_of(near(r))
+        dp_buf[at, :] = times(g_buf[at, :], v_near[...], NT)
+
+    att_near, att_cross, dq_near, dk_near, dk_cross, exchange = [], [], [], [], [], []
+    for step, r in enumerate(order):
+        token = half * groups + near(r)
+        piece = att_all.at[rows_of(token), cols_of(mine)]
+        att_near.append(
+            [
+                remote(
+                    piece, piece, att_send.at[step, n], att_recv.at[step, n],
+                    (half * groups + near(n), h),
+                )
+                for n in range(1, groups)
+            ]
+        )
+        att_cross.append(
+            remote(
+                piece, piece, attx_send.at[step], attx_recv.at[step],
+                ((1 - half) * groups + mine, h),
+            )
+        )
+        if r > 0:
+            dq_near.append(
+                remote(
+                    dq_send.at[r], dq_in.at[:, cols_of(mine)], dq_ssem.at[r], dq_rsem.at[r],
+                    (token, h),
+                )
+            )
+            for n, (src, dst) in enumerate(((dk_send, dk_in), (dv_send, dv_in))):
+                dk_near.append(
+                    remote(
+                        src.at[rows_of(near(r)), :], dst.at[:, cols_of(mine)], dk_ssem.at[r, n],
+                        dk_rsem.at[r, n], (token, h),
+                    )
+                )
+        for n, (src, dst) in enumerate(((dkf_send, dk_back), (dvf_send, dv_back))):
+            dk_cross.append(
+                remote(
+                    src.at[rows_of(near(r)), :], dst.at[:, cols_of(mine)], dkf_ssem.at[r, n],
+                    dkf_rsem.at[r, n], ((1 - half) * groups + near(r), h),
+                )
+            )
+
+    def finish(with_far):
+        for step, r in enumerate(order):
+            block = near(r)
+            at = rows_of(block)
+            qc, gc = q_buf[at, :], g_buf[at, :]
+            scores = s_buf[at, :]
+            largest = jnp.max(scores, axis=1, keepdims=True)
+            if with_far:
+                others = jnp.where(
+                    matching(groups + block, 0), times(qc, k_far[...], NT) * scaling, -1e30
+                )
+                largest = jnp.maximum(largest, jnp.max(others, axis=1, keepdims=True))
+            weights = jnp.exp(scores - largest)
+            total = jnp.sum(weights, axis=1, keepdims=True)
+            if with_far:
+                more = jnp.exp(others - largest)
+                total = total + jnp.sum(more, axis=1, keepdims=True)
+            share = 1.0 / total
+            probs = weights * share
+            rounded = probs.astype(bf)
+            attended = jnp.dot(rounded, v_near[...], preferred_element_type=f32)
+            p_near[at, :] = rounded
+            if with_far:
+                probs_far = more * share
+                rounded_far = probs_far.astype(bf)
+                attended = attended + jnp.dot(
+                    rounded_far, v_far[...], preferred_element_type=f32
+                )
+                p_far[at, :] = rounded_far
+            attended = attended.astype(bf)
+            att_all[rows_of(half * groups + block), cols_of(mine)] = attended
+            att_cross[step].start()
+            for copy in att_near[step]:
+                copy.start()
+            centre = jnp.sum(attended.astype(f32) * gc.astype(f32), axis=1, keepdims=True)
+            ds_near[at, :] = (probs * (dp_buf[at, :] - centre)).astype(bf)
+            if with_far:
+                ds_far[at, :] = (probs_far * (times(gc, v_far[...], NT) - centre)).astype(bf)
+        if with_far:
+            for step, r in enumerate(order):
+                at = rows_of(near(r))
+                dvf_send[at, :] = times(p_far[:, cols_of(near(r), rows)], g_buf[...], TN).astype(bf)
+                dkf_send[at, :] = (
+                    times(ds_far[:, cols_of(near(r), rows)], q_buf[...], TN) * scaling
+                ).astype(bf)
+                dk_cross[2 * step].start()
+                dk_cross[2 * step + 1].start()
+        for step, r in enumerate(order):
+            at = rows_of(near(r))
+            dq = jnp.dot(ds_near[at, :], k_near[...], preferred_element_type=f32)
+            if with_far:
+                dq = dq + jnp.dot(ds_far[at, :], k_far[...], preferred_element_type=f32)
+            dq = (dq * scaling).astype(bf)
+            dv = times(p_near[:, cols_of(near(r), rows)], g_buf[...], TN).astype(bf)
+            dk = (times(ds_near[:, cols_of(near(r), rows)], q_buf[...], TN) * scaling).astype(bf)
+            if r == 0:
+                dq_in[:, cols_of(mine)] = dq
+                dk_in[:, cols_of(mine)] = dk
+                dv_in[:, cols_of(mine)] = dv
+            else:
+                dq_send[r] = dq
+                dk_send[at, :] = dk
+                dv_send[at, :] = dv
+                dq_near[step].start()
+                dk_near[2 * step].start()
+                dk_near[2 * step + 1].start()
+
+    @pl.when(low)
+    def _():
+        finish(False)
+
     @pl.when(high)
     def _():
         for copy in far:
             copy.wait_recv()
-
-    keys_bucket = brow[...]
-    keys_at = lax.broadcasted_iota(jnp.int32, (rows, seqs * rows), 1)
-    exchange = []
-    sent = []
-    att_near = []
-    att_cross = []
-    dq_near = []
-    order = list(range(1, groups)) + [0]
-    for step, r in enumerate(order):
-        block = near(r)
-        token = half * groups + block
-        qc = q_buf[rows_of(block), :]
-        gc = g_buf[rows_of(block), :]
-        k_all = k_buf[...]
-        v_all = v_buf[...]
-        gap = bcol[rows_of(token), :] - keys_bucket
-        query_at = token * rows + lax.broadcasted_iota(jnp.int32, (rows, seqs * rows), 0)
-        allowed = ((gap == 0) | (gap == 1)) & (keys_at <= query_at)
-        scores = jnp.where(allowed, times(qc, k_all, NT) * scaling, -1e30)
-        largest = jnp.max(scores, axis=1, keepdims=True)
-        weights = jnp.where(allowed, jnp.exp(scores - largest), 0.0)
-        probs = weights * (1.0 / jnp.sum(weights, axis=1, keepdims=True))
-        rounded = probs.astype(jnp.bfloat16)
-        attended = jnp.dot(rounded, v_all, preferred_element_type=jnp.float32).astype(jnp.bfloat16)
-        att_all[rows_of(token), cols_of(mine)] = attended
-        for n in range(1, groups):
-            copy = remote(
-                att_all.at[rows_of(token), cols_of(mine)],
-                att_all.at[rows_of(token), cols_of(mine)],
-                att_send.at[step, n], att_recv.at[step, n],
-                (half * groups + near(n), h),
+        finish(True)
+
+    go_own.wait()
+    for copy in spread:
+        copy.wait_recv()
+    level = go_all.at[:, quarter_of(h), :]
+    for m in range(1, pairs):
+        exchange.append(
+            remote(
+                level, level, gx_send.at[m], gx_recv.at[m], (s, lax.rem(h + 2 * m, heads))
             )
-            copy.start()
-            att_near.append(copy)
-        copy = remote(
-            att_all.at[rows_of(token), cols_of(mine)],
-            att_all.at[rows_of(token), cols_of(mine)],
-            attx_send.at[step], attx_recv.at[step], ((1 - half) * groups + mine, h),
-        )
+        )
+        exchange[-1].start()
+    passing = [remote(level, level, gf_send.at[0], gf_recv.at[0], (s, partner))]
+    passing[0].start()
+
+    for copies in att_near:
+        for copy in copies:
+            copy.wait_recv()
+    home = att_all[rows_of(s), :]
+
+    def product(to):
+        return jnp.dot(home, w_buf[:, cols_of(to, lcols)], preferred_element_type=f32)
+
+    def same_core(m):
+        return lax.rem(h + 2 * m, heads)
+
+    def other_core(m):
+        return lax.rem(h - core + 2 * m, heads) + 1 - core
+
+    lo_near = []
+    for m in list(range(1, pairs)) + [0]:
+        lo_send[m] = product(other_core(m)).astype(bf)
+        copy = remote(lo_send.at[m], lo_in.at[m], lo_ssem.at[m], lo_rsem.at[m], (s, partner))
         copy.start()
-        att_cross.append(copy)
-        centre = jnp.sum(
-            attended.astype(jnp.float32) * gc.astype(jnp.float32), axis=1, keepdims=True
-        )
-        dscores = (probs * (times(gc, v_all, NT) - centre)).astype(jnp.bfloat16)
-        dq = (jnp.dot(dscores, k_all, preferred_element_type=jnp.float32) * scaling).astype(
-            jnp.bfloat16
-        )
-        if r == 0:
-            dq_in[:, cols_of(mine)] = dq
-        else:
-            dq_send[r] = dq
-            copy = remote(
-                dq_send.at[r], dq_in.at[:, cols_of(mine)], dq_ssem.at[r], dq_rsem.at[r],
-                (token, h),
-            )
-            copy.start()
-            dq_near.append(copy)
-        dk = times(dscores, qc, TN)
-        dv = times(rounded, gc, TN)
-        if step == 0:
-            dk_acc[...] = dk
-            dv_acc[...] = dv
-        else:
-            dk_acc[...] += dk
-            dv_acc[...] += dv
-        if step == 1:
-            go_own.wait()
-            for copy in spread:
-                copy.wait_recv()
-            for n in range(1, heads):
-                copy = remote(
-                    go_all.at[:, quarter_rows, :], go_all.at[:, quarter_rows, :],
-                    gx_send.at[n], gx_recv.at[n], (s, lax.rem(h + n, heads)),
-                )
-                copy.start()
-                exchange.append(copy)
-
-    dk_send[...] = (dk_acc[...] * scaling).astype(jnp.bfloat16)
-    dv_send[...] = dv_acc[...].astype(jnp.bfloat16)
-    dk_cross = []
-    for r in range(groups):
-        to = near(r)
-        for n, (src, dst) in enumerate(((dk_send, dk_far), (dv_send, dv_far))):
-            dk_cross.append(
-                remote(
-                    src.at[rows_of(to), :], dst.at[:, cols_of(mine)], dkf_ssem.at[r, n],
-                    dkf_rsem.at[r, n], ((1 - half) * groups + to, h),
-                )
-            )
-
-    @pl.when(high)
-    def _():
-        for copy in dk_cross:
-            copy.start()
-
-    dk_near = []
-    for r in range(1, groups):
-        to = near(r)
-        for n, (src, dst) in enumerate(((dk_send, dk_in), (dv_send, dv_in))):
-            copy = remote(
-                src.at[rows_of(half * groups + to), :], dst.at[:, cols_of(mine)],
-                dk_ssem.at[r, n], dk_rsem.at[r, n], (half * groups + to, h),
-            )
-            copy.start()
-            dk_near.append(copy)
-    dk_in[:, cols_of(mine)] = dk_send[rows_of(s), :]
-    dv_in[:, cols_of(mine)] = dv_send[rows_of(s), :]
+        lo_near.append(copy)
 
     for copy in att_cross:
         copy.wait_recv()
@@ -516,35 +595,42 @@
         copy.start()
         forward.append(copy)
 
-    for copy in att_near:
-        copy.wait_recv()
-    home = att_all[rows_of(s), :]
-    lo_near = []
-    for n in range(1, heads):
-        to = lax.rem(h + n, heads)
-        lo_send[n] = jnp.dot(
-            home, w_buf[:, cols_of(to, lcols)], preferred_element_type=jnp.float32
-        ).astype(jnp.bfloat16)
-        copy = remote(lo_send.at[n], lo_in.at[n], lo_ssem.at[n], lo_rsem.at[n], (s, to))
+    sums = []
+    for m in range(1, pairs):
+        mixed = product(same_core(m))
+        lo_near[m - 1].wait_recv()
+        sum_send[m] = (mixed + lo_in[m].astype(f32)).astype(bf)
+        copy = remote(
+            sum_send.at[m], sum_in.at[m], sum_ssem.at[m], sum_rsem.at[m], (s, same_core(m))
+        )
         copy.start()
-        lo_near.append(copy)
-    layer = jnp.dot(home, w_buf[:, cols_of(h, lcols)], preferred_element_type=jnp.float32)
-
-    for copy in exchange:
-        copy.wait_recv()
+        sums.append(copy)
+    layer = product(h)
+
+    for m in range(1, pairs):
+        exchange[m - 1].wait_recv()
+        from_there = go_all.at[:, quarter_of(lax.rem(h + heads - 2 * m, heads)), :]
+        copy = remote(from_there, from_there, gf_send.at[m], gf_recv.at[m], (s, partner))
+        copy.start()
+        passing.append(copy)
+
     for copy in dq_near:
         copy.wait_recv()
     gq_out[...] = dq_in[...]
-    for n, copy in enumerate(lo_near):
+    for copy in passing:
         copy.wait_recv()
-        layer = layer + lo_in[n + 1].astype(jnp.float32)
-    lo_out[...] = layer.astype(jnp.bfloat16)
     for copy in forward:
         copy.wait_recv()
-    gw = jnp.zeros(gw_out.shape, jnp.float32)
+    gw = jnp.zeros(gw_out.shape, f32)
     for c in range(seqs):
         gw = gw + times(att_all[c * rows : (c + 1) * rows, :], go_all[c], TN)
     gw_out[...] = gw
+    lo_near[-1].wait_recv()
+    layer = layer + lo_in[0].astype(f32)
+    for m in range(1, pairs):
+        sums[m - 1].wait_recv()
+        layer = layer + sum_in[m].astype(f32)
+    lo_out[...] = layer.astype(bf)
     for copy in dk_near:
         copy.wait_recv()
 
@@ -553,15 +639,12 @@
         for copy in dk_cross:
             copy.wait_recv()
 
-    gk_out[...] = (dk_in[...].astype(jnp.float32) + dk_far[...].astype(jnp.float32)).astype(
-        jnp.bfloat16
-    )
-    gv_out[...] = (dv_in[...].astype(jnp.float32) + dv_far[...].astype(jnp.float32)).astype(
-        jnp.bfloat16
-    )
+    gk_out[...] = (dk_in[...].astype(f32) + dk_back[...].astype(f32)).astype(bf)
+    gv_out[...] = (dv_in[...].astype(f32) + dv_back[...].astype(f32)).astype(bf)
 
     for copy in (
-        inside + spread + exchange + att_near + att_cross + dq_near + dk_near + forward + lo_near
+        inside + inside_g + spread + exchange + passing + sum(att_near, []) + att_cross + dq_near
+        + dk_near + forward + lo_near + sums
     ):
         copy.wait_send()
 
@@ -574,6 +657,24 @@
     def _():
         for copy in dk_cross:
             copy.wait_send()
+
+
+def hand_over(count, *refs):
+    sources, targets, holds = refs[:count], refs[count : 2 * count], refs[2 * count : 3 * count]
+    sem_in, sem_out = refs[3 * count :]
+    fetched = [
+        pltpu.make_async_copy(a, b, sem_in.at[n]) for n, (a, b) in enumerate(zip(sources, holds))
+    ]
+    written = [
+        pltpu.make_async_copy(a, b, sem_out.at[n]) for n, (a, b) in enumerate(zip(holds, targets))
+    ]
+    for copy in fetched:
+        copy.start()
+    for one, two in zip(fetched, written):
+        one.wait()
+        two.start()
+    for copy in written:
+        copy.wait()
 
 
 def dense_device(queries, keys, values, bucket, w_out, grad_out):
@@ -582,6 +683,7 @@
     rows, features = queries.shape
     model = w_out.shape[1]
     groups = features // HSZ
+    pairs = heads // 2
     part = groups * rows
     tokens = seqs * rows
     bf, f32 = jnp.bfloat16, jnp.float32
@@ -589,55 +691,59 @@
     hbm = pl.BlockSpec(memory_space=pl.ANY)
     dma = pltpu.SemaphoreType.DMA
     wide = pltpu.VMEM((rows, features), bf)
+    tall = pltpu.VMEM((part, HSZ), bf)
+    square = pltpu.VMEM((part, part), bf)
+    layers = pltpu.VMEM((pairs, rows, model // heads), bf)
     sems = []
     for shape in (
-        (groups, 4), (groups, 2), (seqs,), (heads,), (groups, groups), (groups,), (groups,),
-        (groups,), (groups, 2), (groups, 2), (heads,),
+        (groups, 4), (groups, 2), (seqs,), (pairs,), (pairs,), (groups, groups), (groups,),
+        (groups,), (groups,), (groups, 2), (groups, 2), (pairs,), (pairs,),
     ):
         sems += [dma(shape), dma(shape)]
-    return pl.pallas_call(
+    results = (
+        jax.ShapeDtypeStruct((rows, model // heads), bf),
+        jax.ShapeDtypeStruct((rows, features), bf),
+        jax.ShapeDtypeStruct((rows, features), bf),
+        jax.ShapeDtypeStruct((rows, features), bf),
+        jax.ShapeDtypeStruct((features, model // seqs), f32),
+    )
+    outs = pl.pallas_call(
         functools.partial(dense_kernel, seqs, heads),
-        out_shape=(
-            jax.ShapeDtypeStruct((rows, model // heads), bf),
-            jax.ShapeDtypeStruct((rows, features), bf),
-            jax.ShapeDtypeStruct((rows, features), bf),
-            jax.ShapeDtypeStruct((rows, features), bf),
-            jax.ShapeDtypeStruct((features, model // seqs), f32),
-        ),
-        in_specs=[hbm, hbm, hbm, vmem, vmem, hbm, hbm],
+        out_shape=results,
+        in_specs=[hbm, hbm, hbm, vmem, hbm, hbm],
         out_specs=(vmem,) * 5,
         scratch_shapes=[
             pltpu.VMEM(w_out.shape, bf),
             pltpu.VMEM(grad_out.shape, bf),
             wide,
-            pltpu.VMEM((part, HSZ), bf),
-            pltpu.VMEM((part, HSZ), bf),
-            pltpu.VMEM((tokens, HSZ), bf),
-            pltpu.VMEM((tokens, HSZ), bf),
+            *([tall] * 6),
             pltpu.VMEM((seqs, rows, model // seqs), bf),
             pltpu.VMEM((tokens, features), bf),
+            pltpu.VMEM((part, part), f32),
+            pltpu.VMEM((part, part), f32),
+            *([square] * 4),
             pltpu.VMEM((groups, rows, HSZ), bf),
-            pltpu.VMEM((tokens, HSZ), f32),
-            pltpu.VMEM((tokens, HSZ), f32),
-            pltpu.VMEM((tokens, HSZ), bf),
-            pltpu.VMEM((tokens, HSZ), bf),
-            wide,
-            wide,
-            wide,
-            wide,
-            wide,
-            pltpu.VMEM((heads, rows, model // heads), bf),
-            pltpu.VMEM((heads, rows, model // heads), bf),
+            *([tall] * 4),
+            *([wide] * 5),
+            *([layers] * 4),
             dma((6,)),
         ]
         + sems,
         compiler_params=pltpu.CompilerParams(collective_id=0, has_side_effects=True),
-    )(queries, keys, values, bucket, bucket.reshape(1, -1), w_out, grad_out)
+    )(queries, keys, values, bucket.reshape(1, -1), w_out, grad_out)
+    return pl.pallas_call(
+        functools.partial(hand_over, len(results)),
+        out_shape=results,
+        in_specs=[hbm] * len(results),
+        out_specs=(hbm,) * len(results),
+        scratch_shapes=[pltpu.VMEM(r.shape, r.dtype) for r in results]
+        + [dma((len(results),)), dma((len(results),))],
+    )(*outs)
 
 
 def choose(queries, keys, values, bucket, w_out, grad_out):
     groups = queries.shape[1] // HSZ
-    dense = lax.axis_size("seq") == 2 * groups
+    dense = lax.axis_size("seq") == 2 * groups and lax.axis_size("head") % 2 == 0
     plan = dense_device if dense else per_device
     return plan(queries, keys, values, bucket, w_out, grad_out)
 

time: 61.5 us -> 52.2 us (0.85)
  the two profiles are of different devices: /device:TPU:1 before, /device:TPU:0 now
where the time goes in v2:
time: 52.2 us; the launch traced here: 52 us
  Pallas kernels  51.3 us (98%)
  between operations  0.64 us (1%)
    pallas_call x1, Pallas kernels, dense_device(): pl.pallas_call(functools.partial(dense_kernel, seqs, heads), out_shape=re...  48.8 us
    pallas_call x1, Pallas kernels, dense_device(): pl.pallas_call(functools.partial(hand_over, len(results)), out_shape=resu...  2.54 us

profile of v2, /device:TPU:0, one launch (start us, length us, event | category | flops | bytes accessed | tf_op | source)
XLA Modules:
  0.0 52.0 jit_solution(14469863727731938077)
XLA Ops:
  0.6 48.8 %shard_map.101 = (bf16[128,1024]{1,0:T(8,128)(2,1)}, bf16[128,512]{1,0:T(8,128)(2,1)}, bf16[128,512]{1,0:T(8,128)(2,1)}, bf16[128,512]{1,0:T(8,128)(2,1)}, f32[512,512]{1,0:T(8,128)}) custom-call(bf16[128,512]{1,0:T(8,128)(2,1)} %q_hbm.1, bf16[128,512]{1,0:T(8,128)(2,1)} %k_hbm.1, bf16[128,512]{1,0:T(8,128)(2,1)} %v_hbm.1, s32[1,1024]{1,0:T(1,128)} %bitcast.1, ...), custom_call_target="tpu_custom_call" | custom-call | tf_op jit(solution)/shard_map/pallas_call | solution.py:710
  49.4 2.5 %shard_map.102 = (bf16[128,1024]{1,0:T(8,128)(2,1)}, bf16[128,512]{1,0:T(8,128)(2,1)}, bf16[128,512]{1,0:T(8,128)(2,1)}, bf16[128,512]{1,0:T(8,128)(2,1)}, f32[512,512]{1,0:T(8,128)}) custom-call(bf16[128,1024]{1,0:T(8,128)(2,1)} %get-tuple-element.10.refs_0_, bf16[128,512]{1,0:T(8,128)(2,1)} %get-tuple-element.11.refs_1_, ...), custom_call_target="tpu_custom_call" | custom-call | tf_op jit(solution)/shard_map/pallas_call | solution.py:734

commit v3 on v2

--- a/solution.py
+++ b/solution.py
@@ -257,8 +257,12 @@
     att_recv,
     attx_send,
     attx_recv,
+    rel_send,
+    rel_recv,
     fwd_send,
     fwd_recv,
+    far_rel_send,
+    far_rel_recv,
     dq_ssem,
     dq_rsem,
     dk_ssem,
@@ -377,17 +381,18 @@
         return total + times(go_buf[:, at], w_buf[:, at], NT)
 
     gh = lax.fori_loop(0, seqs, heads_step, jnp.zeros((rows, groups * width), f32))
-    gh_buf[...] = gh.astype(bf)
+    for j in range(groups):
+        gh_buf[j] = gh[:, j * width : (j + 1) * width].astype(bf)
     inside_g = []
     for r in range(1, groups):
         to = near(r)
         copy = remote(
-            gh_buf.at[:, cols_of(to)], g_buf.at[rows_of(mine), :], in_send.at[r, 3],
+            gh_buf.at[to], g_buf.at[rows_of(mine), :], in_send.at[r, 3],
             in_recv.at[r, 3], (half * groups + to, h),
         )
         copy.start()
         inside_g.append(copy)
-    g_buf[rows_of(mine), :] = gh_buf[:, cols_of(mine)]
+    g_buf[rows_of(mine), :] = gh_buf[mine]
 
     spread = []
     for r in range(1, seqs):
@@ -430,17 +435,19 @@
         at = rows_of(near(r))
         dp_buf[at, :] = times(g_buf[at, :], v_near[...], NT)
 
+    across = mine + 1 - 2 * lax.rem(mine, 2)
+    beside = [across] + [near(2 * k) for k in range(1, groups // 2)]
     att_near, att_cross, dq_near, dk_near, dk_cross, exchange = [], [], [], [], [], []
     for step, r in enumerate(order):
         token = half * groups + near(r)
-        piece = att_all.at[rows_of(token), cols_of(mine)]
+        piece = att_all.at[mine, rows_of(token), :]
         att_near.append(
             [
                 remote(
                     piece, piece, att_send.at[step, n], att_recv.at[step, n],
-                    (half * groups + near(n), h),
+                    (half * groups + to, h),
                 )
-                for n in range(1, groups)
+                for n, to in enumerate(beside)
             ]
         )
         att_cross.append(
@@ -452,21 +459,21 @@
         if r > 0:
             dq_near.append(
                 remote(
-                    dq_send.at[r], dq_in.at[:, cols_of(mine)], dq_ssem.at[r], dq_rsem.at[r],
+                    dq_send.at[r], dq_in.at[mine], dq_ssem.at[r], dq_rsem.at[r],
                     (token, h),
                 )
             )
             for n, (src, dst) in enumerate(((dk_send, dk_in), (dv_send, dv_in))):
                 dk_near.append(
                     remote(
-                        src.at[rows_of(near(r)), :], dst.at[:, cols_of(mine)], dk_ssem.at[r, n],
+                        src.at[rows_of(near(r)), :], dst.at[mine], dk_ssem.at[r, n],
                         dk_rsem.at[r, n], (token, h),
                     )
                 )
         for n, (src, dst) in enumerate(((dkf_send, dk_back), (dvf_send, dv_back))):
             dk_cross.append(
                 remote(
-                    src.at[rows_of(near(r)), :], dst.at[:, cols_of(mine)], dkf_ssem.at[r, n],
+                    src.at[rows_of(near(r)), :], dst.at[mine], dkf_ssem.at[r, n],
                     dkf_rsem.at[r, n], ((1 - half) * groups + near(r), h),
                 )
             )
@@ -501,7 +508,7 @@
                 )
                 p_far[at, :] = rounded_far
             attended = attended.astype(bf)
-            att_all[rows_of(half * groups + block), cols_of(mine)] = attended
+            att_all[mine, rows_of(half * groups + block), :] = attended
             att_cross[step].start()
             for copy in att_near[step]:
                 copy.start()
@@ -527,9 +534,9 @@
             dv = times(p_near[:, cols_of(near(r), rows)], g_buf[...], TN).astype(bf)
             dk = (times(ds_near[:, cols_of(near(r), rows)], q_buf[...], TN) * scaling).astype(bf)
             if r == 0:
-                dq_in[:, cols_of(mine)] = dq
-                dk_in[:, cols_of(mine)] = dk
-                dv_in[:, cols_of(mine)] = dv
+                dq_in[mine] = dq
+                dk_in[mine] = dk
+                dv_in[mine] = dv
             else:
                 dq_send[r] = dq
                 dk_send[at, :] = dk
@@ -562,10 +569,34 @@
     passing = [remote(level, level, gf_send.at[0], gf_recv.at[0], (s, partner))]
     passing[0].start()
 
+    ours = pl.ds(pl.multiple_of(half * part, part), part)
+    theirs = pl.ds(pl.multiple_of((1 - half) * part, part), part)
+
+    def block_of(where, column):
+        return att_all.at[column, where, :]
+
+    relay = []
+    for k in range(1, groups // 2):
+        for copies in att_near:
+            copies[k].wait_recv()
+        block = block_of(ours, near(groups - 2 * k))
+        relay.append(
+            remote(block, block, rel_send.at[k], rel_recv.at[k], (half * groups + across, h))
+        )
+        relay[-1].start()
+    for copy in att_cross:
+        copy.wait_recv()
+    forward = []
+    for n, to in reversed(list(enumerate(beside))):
+        block = block_of(theirs, mine)
+        copy = remote(block, block, fwd_send.at[n], fwd_recv.at[n], (half * groups + to, h))
+        copy.start()
+        forward.append(copy)
     for copies in att_near:
-        for copy in copies:
-            copy.wait_recv()
-    home = att_all[rows_of(s), :]
+        copies[0].wait_recv()
+    for copy in relay:
+        copy.wait_recv()
+    home = jnp.concatenate([att_all[j, rows_of(s), :] for j in range(groups)], axis=1)
 
     def product(to):
         return jnp.dot(home, w_buf[:, cols_of(to, lcols)], preferred_element_type=f32)
@@ -582,18 +613,6 @@
         copy = remote(lo_send.at[m], lo_in.at[m], lo_ssem.at[m], lo_rsem.at[m], (s, partner))
         copy.start()
         lo_near.append(copy)
-
-    for copy in att_cross:
-        copy.wait_recv()
-    forward = []
-    theirs = pl.ds(pl.multiple_of((1 - half) * part, part), part)
-    for n in range(1, groups):
-        copy = remote(
-            att_all.at[theirs, cols_of(mine)], att_all.at[theirs, cols_of(mine)],
-            fwd_send.at[n], fwd_recv.at[n], (half * groups + near(n), h),
-        )
-        copy.start()
-        forward.append(copy)
 
     sums = []
     for m in range(1, pairs):
@@ -614,17 +633,37 @@
         copy.start()
         passing.append(copy)
 
+    far_relay = []
+    for k in range(1, groups // 2):
+        forward[groups // 2 - 1 - k].wait_recv()
+        block = block_of(theirs, near(groups - 2 * k))
+        far_relay.append(
+            remote(
+                block, block, far_rel_send.at[k], far_rel_recv.at[k],
+                (half * groups + across, h),
+            )
+        )
+        far_relay[-1].start()
+
     for copy in dq_near:
         copy.wait_recv()
-    gq_out[...] = dq_in[...]
+    for j in range(groups):
+        gq_out[:, j * width : (j + 1) * width] = dq_in[j]
     for copy in passing:
         copy.wait_recv()
-    for copy in forward:
+
+    def weigh(which):
+        at = pl.ds(pl.multiple_of(which * part, part), part)
+        grads = go_all[pl.ds(which * groups, groups)].reshape(part, gcols)
+        return [times(att_all[j, at, :], grads, TN) for j in range(groups)]
+
+    for j, term in enumerate(weigh(half)):
+        gw_out[j * width : (j + 1) * width, :] = term
+    forward[-1].wait_recv()
+    for copy in far_relay:
         copy.wait_recv()
-    gw = jnp.zeros(gw_out.shape, f32)
-    for c in range(seqs):
-        gw = gw + times(att_all[c * rows : (c + 1) * rows, :], go_all[c], TN)
-    gw_out[...] = gw
+    for j, term in enumerate(weigh(1 - half)):
+        gw_out[j * width : (j + 1) * width, :] += term
     lo_near[-1].wait_recv()
     layer = layer + lo_in[0].astype(f32)
     for m in range(1, pairs):
@@ -639,12 +678,14 @@
         for copy in dk_cross:
             copy.wait_recv()
 
-    gk_out[...] = (dk_in[...].astype(f32) + dk_back[...].astype(f32)).astype(bf)
-    gv_out[...] = (dv_in[...].astype(f32) + dv_back[...].astype(f32)).astype(bf)
+    for j in range(groups):
+        at = slice(j * width, (j + 1) * width)
+        gk_out[:, at] = (dk_in[j].astype(f32) + dk_back[j].astype(f32)).astype(bf)
+        gv_out[:, at] = (dv_in[j].astype(f32) + dv_back[j].astype(f32)).astype(bf)
 
     for copy in (
         inside + inside_g + spread + exchange + passing + sum(att_near, []) + att_cross + dq_near
-        + dk_near + forward + lo_near + sums
+        + dk_near + relay + forward + far_relay + lo_near + sums
     ):
         copy.wait_send()
 
@@ -659,15 +700,15 @@
             copy.wait_send()
 
 
-def hand_over(count, *refs):
+def hand_over(count, piece, *refs):
     sources, targets, holds = refs[:count], refs[count : 2 * count], refs[2 * count : 3 * count]
     sem_in, sem_out = refs[3 * count :]
-    fetched = [
-        pltpu.make_async_copy(a, b, sem_in.at[n]) for n, (a, b) in enumerate(zip(sources, holds))
-    ]
-    written = [
-        pltpu.make_async_copy(a, b, sem_out.at[n]) for n, (a, b) in enumerate(zip(holds, targets))
-    ]
+    fetched, written = [], []
+    for a, b, c in zip(sources, holds, targets):
+        for start in range(0, a.shape[0], piece):
+            at, n = pl.ds(start, piece), len(fetched)
+            fetched.append(pltpu.make_async_copy(a.at[at], b.at[at], sem_in.at[n]))
+            written.append(pltpu.make_async_copy(b.at[at], c.at[at], sem_out.at[n]))
     for copy in fetched:
         copy.start()
     for one, two in zip(fetched, written):
@@ -690,14 +731,14 @@
     vmem = pl.BlockSpec(memory_space=pltpu.VMEM)
     hbm = pl.BlockSpec(memory_space=pl.ANY)
     dma = pltpu.SemaphoreType.DMA
-    wide = pltpu.VMEM((rows, features), bf)
+    piled = pltpu.VMEM((groups, rows, HSZ), bf)
     tall = pltpu.VMEM((part, HSZ), bf)
     square = pltpu.VMEM((part, part), bf)
     layers = pltpu.VMEM((pairs, rows, model // heads), bf)
     sems = []
     for shape in (
         (groups, 4), (groups, 2), (seqs,), (pairs,), (pairs,), (groups, groups), (groups,),
-        (groups,), (groups,), (groups, 2), (groups, 2), (pairs,), (pairs,),
+        (groups,), (groups,), (groups,), (groups,), (groups, 2), (groups, 2), (pairs,), (pairs,),
     ):
         sems += [dma(shape), dma(shape)]
     results = (
@@ -707,6 +748,7 @@
         jax.ShapeDtypeStruct((rows, features), bf),
         jax.ShapeDtypeStruct((features, model // seqs), f32),
     )
+    pieces = sum(r.shape[0] // rows for r in results)
     outs = pl.pallas_call(
         functools.partial(dense_kernel, seqs, heads),
         out_shape=results,
@@ -715,16 +757,16 @@
         scratch_shapes=[
             pltpu.VMEM(w_out.shape, bf),
             pltpu.VMEM(grad_out.shape, bf),
-            wide,
+            piled,
             *([tall] * 6),
             pltpu.VMEM((seqs, rows, model // seqs), bf),
-            pltpu.VMEM((tokens, features), bf),
+            pltpu.VMEM((groups, tokens, HSZ), bf),
             pltpu.VMEM((part, part), f32),
             pltpu.VMEM((part, part), f32),
             *([square] * 4),
             pltpu.VMEM((groups, rows, HSZ), bf),
             *([tall] * 4),
-            *([wide] * 5),
+            *([piled] * 5),
             *([layers] * 4),
             dma((6,)),
         ]
@@ -732,18 +774,18 @@
         compiler_params=pltpu.CompilerParams(collective_id=0, has_side_effects=True),
     )(queries, keys, values, bucket.reshape(1, -1), w_out, grad_out)
     return pl.pallas_call(
-        functools.partial(hand_over, len(results)),
+        functools.partial(hand_over, len(results), rows),
         out_shape=results,
         in_specs=[hbm] * len(results),
         out_specs=(hbm,) * len(results),
         scratch_shapes=[pltpu.VMEM(r.shape, r.dtype) for r in results]
-        + [dma((len(results),)), dma((len(results),))],
+        + [dma((pieces,)), dma((pieces,))],
     )(*outs)
 
 
 def choose(queries, keys, values, bucket, w_out, grad_out):
     groups = queries.shape[1] // HSZ
-    dense = lax.axis_size("seq") == 2 * groups and lax.axis_size("head") % 2 == 0
+    dense = lax.axis_size("seq") == 2 * groups and lax.axis_size("head") % 2 == 0 and groups % 2 == 0
     plan = dense_device if dense else per_device
     return plan(queries, keys, values, bucket, w_out, grad_out)
 

time: 52.2 us -> 51.2 us (0.981); the launches traced: 52 us -> 50.4 us
  Pallas kernels: 51.3 us -> 49.8 us
    pallas_call x1, Pallas kernels: 48.8 us -> 47.5 us  [dense_device(): pl.pallas_call(functools.partial(dense_kernel, seqs, heads), out_shape=re...]
where the time goes in v3:
time: 51.2 us; the launch traced here: 50.4 us
  Pallas kernels  49.8 us (97%)
  between operations  0.64 us (1%)
    pallas_call x1, Pallas kernels, dense_device(): pl.pallas_call(functools.partial(dense_kernel, seqs, heads), out_shape=re...  47.5 us
    pallas_call x1, Pallas kernels, dense_device(): pl.pallas_call(functools.partial(hand_over, len(results), rows), out_shap...  2.3 us

profile of v3, /device:TPU:0, one launch (start us, length us, event | category | flops | bytes accessed | tf_op | source)
XLA Modules:
  0.0 50.4 jit_solution(8361816153445649308)
XLA Ops:
  0.6 47.5 %shard_map.101 = (bf16[128,1024]{1,0:T(8,128)(2,1)}, bf16[128,512]{1,0:T(8,128)(2,1)}, bf16[128,512]{1,0:T(8,128)(2,1)}, bf16[128,512]{1,0:T(8,128)(2,1)}, f32[512,512]{1,0:T(8,128)}) custom-call(bf16[128,512]{1,0:T(8,128)(2,1)} %q_hbm.1, bf16[128,512]{1,0:T(8,128)(2,1)} %k_hbm.1, bf16[128,512]{1,0:T(8,128)(2,1)} %v_hbm.1, s32[1,1024]{1,0:T(1,128)} %bitcast.1, ...), custom_call_target="tpu_custom_call" | custom-call | tf_op jit(solution)/shard_map/pallas_call | solution.py:752
  48.1 2.3 %shard_map.102 = (bf16[128,1024]{1,0:T(8,128)(2,1)}, bf16[128,512]{1,0:T(8,128)(2,1)}, bf16[128,512]{1,0:T(8,128)(2,1)}, bf16[128,512]{1,0:T(8,128)(2,1)}, f32[512,512]{1,0:T(8,128)}) custom-call(bf16[128,1024]{1,0:T(8,128)(2,1)} %get-tuple-element.10.refs_0_, bf16[128,512]{1,0:T(8,128)(2,1)} %get-tuple-element.11.refs_1_, ...), custom_call_target="tpu_custom_call" | custom-call | tf_op jit(solution)/shard_map/pallas_call | solution.py:776
